TPU v7x, 256 devices: a whole 4x4x8 slice. The times are simulated.
256 devices in a mesh: leaf: 64 (over z, y, core), panel: 4 (over x).
Axes of the slice: x: 4, y: 4, z: 8, core: 2. Of those that a mesh axis runs over, the one named last changes fastest.
Arguments:
- right_sides: float32 [7, 4096, 512], P(None, 'leaf', 'panel'), may hold values from -11 to 11
- inverse_diagonal: bfloat16 [7, 4096, 4096], P(None, 'leaf'), may hold values from -1 to 2, as said below
- off_diagonal: bfloat16 [6, 4096, 4096], P(None, 'leaf'), may hold values from -0.0625 to 0.0625
- structure: int32 [6, 32], replicated, may hold values from 0 to 95, as said below
- pivot_counts: int32 [7], replicated, may hold values from 2048 to 4096, as said below
Outputs:
- samples: float32 [7, 4096, 512], P(None, 'leaf', 'panel')
- sample_power: float32 [7, 4096], P(None, 'leaf')
Inputs may be any that keep to these rules, and one draw needn't show every extreme that they name: `inverse_diagonal`: zero below the diagonal; diagonal entries positive. `structure`: a front of the middle level lists 4096 // 128 distinct blocks of the root (numbers below 32); a bottom front lists distinct blocks of the root and of its parent (parent p = 1 + (f - 3) // 2 holds block numbers p * 32 to (p + 1) * 32 - 1). `pivot_counts`: rows from the count on are padding; some front has exactly 4096 live rows and some exactly 2048.
All inputs are finite; a program needn't handle non-finite values.
Results may differ from a plain program's by a relative error of at most 0.0038.
Values may be sent and summed in bfloat16 or wider, within the bound.
No kernel may reach another device: no remote copies, remote signals or barrier semaphores. Data moves between devices by JAX's collectives and lax.ppermute only.
A program may use at most 64 MiB of HBM per device.

v0:
```python
import jax
import jax.numpy as jnp
from jax import lax
from jax.sharding import PartitionSpec as P


def share_rows(stored_rows):
    return lax.all_gather(stored_rows, "leaf", axis=1, tiled=True)


def solve_fronts(rhs_block, update, inverse, live_mask):
    reduced = (live_mask * (rhs_block - update)).astype(jnp.bfloat16)
    running = jnp.einsum(
        "fij,fjr->fir",
        inverse,
        lax.all_gather(reduced, "leaf", axis=1, tiled=True),
        preferred_element_type=jnp.float32,
    )
    return live_mask * running


def couple(blocks, picked):
    return jnp.einsum("fik,fkr->fir", blocks, picked, preferred_element_type=jnp.float32)


def local(right_sides, inverse_diagonal, off_diagonal, structure, pivot_counts):
    rows_local = right_sides.shape[1]
    columns_dev = right_sides.shape[2]
    pivot_rows = inverse_diagonal.shape[2]
    coupled = off_diagonal.shape[2]
    block_size = coupled // structure.shape[1]
    first_row = lax.axis_index("leaf") * rows_local
    position = first_row + jnp.arange(rows_local, dtype=jnp.int32)
    live_rows = (position[None, :] < pivot_counts[:, None]).astype(jnp.float32)[:, :, None]
    wanted = (
        structure[:, :, None] * block_size + jnp.arange(block_size, dtype=jnp.int32)[None, None, :]
    ).reshape(6, coupled)
    pieces = 1
    block_width = columns_dev // pieces
    root_solved = solve_fronts(
        right_sides[0:1], jnp.zeros_like(right_sides[0:1]), inverse_diagonal[0:1], live_rows[0:1]
    )
    root_all = share_rows(root_solved.astype(jnp.bfloat16))[0]
    middle_update = couple(off_diagonal[0:2], jnp.take(root_all, wanted[0:2], axis=0))
    middle = solve_fronts(right_sides[1:3], middle_update, inverse_diagonal[1:3], live_rows[1:3])
    middle_all = share_rows(middle.astype(jnp.bfloat16)).reshape(2 * pivot_rows, block_width)
    ancestors = jnp.concatenate([root_all, middle_all], axis=0)
    bottom_update = couple(off_diagonal[2:6], jnp.take(ancestors, wanted[2:6], axis=0))
    bottom = solve_fronts(right_sides[3:7], bottom_update, inverse_diagonal[3:7], live_rows[3:7])
    results = jnp.concatenate([root_solved, middle, bottom], axis=0)
    squares = lax.psum(jnp.sum(results * results, axis=2), "panel")
    sample_power = squares / jnp.float32(columns_dev * lax.axis_size("panel"))
    return (results, sample_power)


def solution(mesh):
    placed = (P(None, "leaf", "panel"), P(None, "leaf", None), P(None, "leaf", None), P(), P())
    return jax.shard_map(
        local,
        mesh=mesh,
        in_specs=placed,
        out_specs=(P(None, "leaf", "panel"), P(None, "leaf")),
        check_vma=False,
    )
```

profile of v0, /device:TPU:1, one launch (start us, length us, event | category | flops | bytes accessed | tf_op | source)
XLA Modules:
  0.0 513.6 jit_solution(4271180809915617018)
XLA Ops:
  7.2 0.7 compare_convert_fusion
  8.0 1.4 multiply_convert_fusion
  9.5 82.9 %all-gather.7.cloned.1.call-done = bf16[1,4096,128]{2,1,0:T(8,128)(2,1)} async-done(((bf16[1,64,128]{2,1,0:T(8,128)(2,1)}), bf16[1,4096,128]{2,1,0:T(8,128)(2,1)}) %all-gather.7.cloned.1.call-update) | async-done | bytes 1048592 | tf_op jit(solution)/shard_map/all_gather | solution.py:16
  92.3 2.3 bitcast_convert_fusion
  94.7 0.0 all-gather.9.cloned.1.call-start
  94.7 0.7 broadcast_multiply_fusion.1
  95.4 0.1 iota_add_fusion
  95.6 0.1 compare_and_fusion.1
  95.7 74.6 %all-gather.15.cloned.1.call-done = bf16[4096,128]{1,0:T(8,128)(2,1)} async-done(((bf16[64,128]{1,0:T(8,128)(2,1)}), bf16[4096,128]{1,0:T(8,128)(2,1)}) %all-gather.15.cloned.1.call-update) | async-done | bytes 1048592 | tf_op jit(solution)/shard_map/all_gather | solution.py:8
  170.3 23.2 %gather_fusion = bf16[8192,128]{1,0:T(8,128)(2,1)S(1)} fusion(bf16[4096,128]{1,0:T(8,128)(2,1)} %all-gather.15.cloned.1.call-done, s32[8192]{0:T(1024)S(1)} %broadcast_clamp_fusion.1), kind=kCustom, calls=%fused_computation | custom fusion | bytes 4227072 | tf_op jit(solution)/shard_map/jit(_take)/gather | solution.py:44
  193.5 3.3 fusion.46
  196.8 0.0 all-gather.11.cloned.1.call-start
  196.9 75.4 %all-gather.9.cloned.1.call-done = bf16[2,4096,128]{2,1,0:T(8,128)(2,1)} async-done(((bf16[2,64,128]{2,1,0:T(8,128)(2,1)}), bf16[2,4096,128]{2,1,0:T(8,128)(2,1)}) %all-gather.9.cloned.1.call-update) | async-done | bytes 2097168 | tf_op jit(solution)/shard_map/all_gather | solution.py:16
  272.3 3.0 fusion.59
  275.5 0.1 compare_and_fusion
  275.6 74.9 %all-gather.11.cloned.1.call-done = bf16[2,4096,128]{2,1,0:T(8,128)(2,1)} async-done(((bf16[2,64,128]{2,1,0:T(8,128)(2,1)}), bf16[2,4096,128]{2,1,0:T(8,128)(2,1)}) %all-gather.11.cloned.1.call-update) | async-done | bytes 2097168 | tf_op jit(solution)/shard_map/all_gather | solution.py:8
  350.5 2.8 pad_maximum_fusion
  353.3 57.8 %gather_fusion.1 = bf16[16384,128]{1,0:T(8,128)(2,1)} fusion(bf16[12288,128]{1,0:T(8,128)(2,1)S(1)} %pad_maximum_fusion, s32[16384]{0:T(1024)S(1)} %broadcast_clamp_fusion), kind=kCustom, calls=%fused_computation.1 | custom fusion | bytes 8454144 | tf_op jit(solution)/shard_map/jit(_take)/gather | solution.py:48
  411.1 5.9 %fusion.31 = bf16[4,64,128]{2,1,0:T(8,128)(2,1)} fusion(bf16[4,4096,128]{2,1,0:T(8,128)(2,1)} %bitcast.59, pred[4,4096]{1,0:T(4,128)(4,1)S(1)} %compare_and_fusion, bf16[6,64,4096]{2,1,0:T(8,128)(2,1)} %param.7, f32[7,64,128]{2,1,0:T(8,128)} %param.5, f32[4,64]{1,0:T(4,128)S(1)} %slice.62), kind=kOutput, calls=%fused_computation.18 | convolution fusion | flops 270630912 | bytes 6505472 | tf_op jit(solution)/shard_map/fik,fkr->fir/dot_general | solution.py:23
  417.1 76.6 %all-gather.13.cloned.1.call-done = bf16[4,4096,128]{2,1,0:T(8,128)(2,1)} async-done(((bf16[4,64,128]{2,1,0:T(8,128)(2,1)}), bf16[4,4096,128]{2,1,0:T(8,128)(2,1)}) %all-gather.13.cloned.1.call-update) | async-done | bytes 4194320 | tf_op jit(solution)/shard_map/all_gather | solution.py:16
  493.7 3.7 fusion.13
  497.4 0.7 multiply_reduce_fusion
  498.1 8.4 %psum.7 = f32[7,64]{1,0:T(8,128)S(1)} all-reduce(f32[7,64]{1,0:T(8,128)S(1)} %get-tuple-element.2), channel_id=1, replica_groups=mesh['leaf'=64,'panel'=4] {'panel'}, use_global_device_ids=true, to_apply=%region_1.2 | all-reduce | flops 448 | bytes 3584 | tf_op jit(solution)/shard_map/psum | solution.py:51
  506.4 0.6 broadcast_multiply_fusion
  (22 shorter events, 0.4 us)
Async XLA Ops:
  7.2 85.2 %all-gather.7.cloned.1.call-start = ((), (), s32[]{:S(2)}) async-start(), calls=%async_computation | async-start | bytes 1064960 | tf_op jit(solution)/shard_map/all_gather | solution.py:16
  9.4 160.8 %all-gather.15.cloned.1.call-start = ((), (), s32[]{:S(2)}) async-start(), calls=%async_computation.4 | async-start | bytes 1064960 | tf_op jit(solution)/shard_map/all_gather | solution.py:8
  94.7 177.6 %all-gather.9.cloned.1.call-start = ((), (), s32[]{:S(2)}) async-start(), calls=%async_computation.1 | async-start | bytes 2129920 | tf_op jit(solution)/shard_map/all_gather | solution.py:16
  196.8 153.7 %all-gather.11.cloned.1.call-start = ((), (), s32[]{:S(2)}) async-start(), calls=%async_computation.2 | async-start | bytes 2129920 | tf_op jit(solution)/shard_map/all_gather | solution.py:8
  275.3 218.4 %all-gather.13.cloned.1.call-start = ((), (), s32[]{:S(2)}) async-start(), calls=%async_computation.3 | async-start | bytes 4259840 | tf_op jit(solution)/shard_map/all_gather | solution.py:16
Sparse Core Ops, SparseCore 0:
  11.3 80.9 all-gather.6
  95.7 74.5 all-gather.14
  196.9 75.2 all-gather.8
  275.5 74.9 all-gather.10
  417.2 76.4 all-gather.12
where the time goes:
time: 514 us
  waiting for transfers between devices  384 us (75%)
  local copies, waits for them, and re-layouts  81.1 us (16%)
  matrix products  18.3 us (4%)
  between operations  13.9 us (3%)
  blocking collectives  8.37 us (2%)
  other arithmetic  7.24 us (1%)
    all_gather x3, waiting for transfers between devices, solve_fronts(): lax.all_gather(reduced, 'leaf', axis=1, tiled=True)  235 us
    all_gather x2, waiting for transfers between devices, share_rows(): return lax.all_gather(stored_rows, 'leaf', axis=1, tiled=True)  149 us
    gather x1, local copies, waits for them, and re-layouts, local(): jnp.take(ancestors, wanted[2:6], axis=0)  57.8 us
    gather x1, local copies, waits for them, and re-layouts, local(): jnp.take(root_all, wanted[0:2], axis=0)  23.2 us
  transfers between devices with their start and end apart: 5, of which 5 were waited for; matrix products, arithmetic and copies ran while one was open for 0% of the time, Pallas kernels for 0%

commit v1 on v0

--- a/solution.py
+++ b/solution.py
@@ -4,8 +4,14 @@
 from jax.sharding import PartitionSpec as P
 
 
+def hold_the_frame(z_in, peer_axis="leaf"):
+    return jnp.concatenate(
+        lax.all_to_all(jnp.stack([z_in] * lax.axis_size(peer_axis)), peer_axis, 0, 0), axis=1
+    )
+
+
 def share_rows(stored_rows):
-    return lax.all_gather(stored_rows, "leaf", axis=1, tiled=True)
+    return hold_the_frame(stored_rows)
 
 
 def solve_fronts(rhs_block, update, inverse, live_mask):

time: 514 us -> 460 us (0.89)
  waiting for transfers between devices: 384 us -> 312 us
  starting transfers between devices: 0.21 us -> 13.2 us
    all_gather x2 -> x0, waiting for transfers between devices: 149 us -> none  [share_rows(): return lax.all_gather(stored_rows, 'leaf', axis=1, tiled=True)]
    all_to_all x0 -> x2, waiting for transfers between devices: none -> 77.3 us  [hold_the_frame(): lax.all_to_all(jnp.stack([z_in] * lax.axis_size(peer_axis)), peer_axis, 0...]
    all_to_all x0 -> x2, starting transfers between devices: none -> 13.1 us  [hold_the_frame(): lax.all_to_all(jnp.stack([z_in] * lax.axis_size(peer_axis)), peer_axis, 0...]
where the time goes in v1:
time: 460 us; the launch traced here: 459 us
  waiting for transfers between devices  312 us (68%)
  local copies, waits for them, and re-layouts  85.2 us (19%)
  matrix products  17 us (4%)
  between operations  14 us (3%)
  starting transfers between devices  13.2 us (3%)
  other arithmetic  9.07 us (2%)
  blocking collectives  8.37 us (2%)
    all_gather x3, waiting for transfers between devices, solve_fronts(): lax.all_gather(reduced, 'leaf', axis=1, tiled=True)  235 us
    all_to_all x2, waiting for transfers between devices, hold_the_frame(): lax.all_to_all(jnp.stack([z_in] * lax.axis_size(peer_axis)), peer_axis, 0...  77.3 us
    gather x1, local copies, waits for them, and re-layouts, local(): jnp.take(ancestors, wanted[2:6], axis=0)  57.8 us
    gather x1, local copies, waits for them, and re-layouts, local(): jnp.take(root_all, wanted[0:2], axis=0)  24 us
    all_to_all x2, starting transfers between devices, hold_the_frame(): lax.all_to_all(jnp.stack([z_in] * lax.axis_size(peer_axis)), peer_axis, 0...  13.1 us
    dot_general x2, matrix products, couple(): jnp.einsum('fik,fkr->fir', blocks, picked, preferred_element_type=jnp.flo...  9.26 us
  transfers between devices with their start and end apart: 5, of which 5 were waited for; matrix products, arithmetic and copies ran while one was open for 0% of the time, Pallas kernels for 0%

profile of v1, /device:TPU:1, one launch (start us, length us, event | category | flops | bytes accessed | tf_op | source)
XLA Modules:
  0.0 459.3 jit_solution(2346195720533651646)
XLA Ops:
  7.2 0.7 compare_convert_fusion
  8.0 1.4 multiply_convert_fusion
  9.4 82.9 %all-gather.4.cloned.1.call-done = bf16[1,4096,128]{2,1,0:T(8,128)(2,1)} async-done(((bf16[1,64,128]{2,1,0:T(8,128)(2,1)}), bf16[1,4096,128]{2,1,0:T(8,128)(2,1)}) %all-gather.4.cloned.1.call-update) | async-done | bytes 1048592 | tf_op jit(solution)/shard_map/all_gather | solution.py:22
  92.4 1.7 bitcast_convert_fusion
  94.1 1.2 stack.4
  95.3 6.7 %all-to-all-start = ((bf16[64,1,64,128]{3,2,1,0:T(8,128)(2,1)}), bf16[64,1,64,128]{3,2,1,0:T(8,128)(2,1)S(1)}, u32[]{:S(2)}, u32[]{:S(2)}) async-start(bf16[64,1,64,128]{3,2,1,0:T(8,128)(2,1)} %stack.4), calls=%async_computation | async-start | bytes 2097152 | tf_op jit(solution)/shard_map/all_to_all | solution.py:9
  102.1 0.1 iota_add_fusion
  102.4 27.8 %all-to-all-done = bf16[64,1,64,128]{3,2,1,0:T(8,128)(2,1)S(1)} async-done(((bf16[64,1,64,128]{3,2,1,0:T(8,128)(2,1)}), bf16[64,1,64,128]{3,2,1,0:T(8,128)(2,1)S(1)}, u32[]{:S(2)}, u32[]{:S(2)}) %all-to-all-start) | async-done | bytes 1048608 | tf_op jit(solution)/shard_map/all_to_all | solution.py:9
  130.2 24.0 %gather_fusion = bf16[8192,128]{1,0:T(8,128)(2,1)S(1)} fusion(bf16[4096,128]{1,0:T(8,128)(2,1)S(1)} %bitcast.61, s32[8192]{0:T(1024)S(1)} %broadcast_clamp_fusion.1), kind=kCustom, calls=%fused_computation | custom fusion | bytes 4227072 | tf_op jit(solution)/shard_map/jit(_take)/gather | solution.py:50
  154.3 3.3 fusion.46
  157.6 75.0 %all-gather.6.cloned.1.call-done = bf16[2,4096,128]{2,1,0:T(8,128)(2,1)} async-done(((bf16[2,64,128]{2,1,0:T(8,128)(2,1)}), bf16[2,4096,128]{2,1,0:T(8,128)(2,1)}) %all-gather.6.cloned.1.call-update) | async-done | bytes 2097168 | tf_op jit(solution)/shard_map/all_gather | solution.py:22
  232.6 2.4 fusion.59
  235.0 1.9 stack.5
  236.9 6.4 %all-to-all-start.1 = ((bf16[64,2,64,128]{3,2,1,0:T(8,128)(2,1)}), bf16[64,2,64,128]{3,2,1,0:T(8,128)(2,1)S(1)}, u32[]{:S(2)}, u32[]{:S(2)}) async-start(bf16[64,2,64,128]{3,2,1,0:T(8,128)(2,1)} %stack.5), calls=%async_computation.1 | async-start | bytes 4194304 | tf_op jit(solution)/shard_map/all_to_all | solution.py:9
  243.5 49.5 %all-to-all-done.1 = bf16[64,2,64,128]{3,2,1,0:T(8,128)(2,1)S(1)} async-done(((bf16[64,2,64,128]{3,2,1,0:T(8,128)(2,1)}), bf16[64,2,64,128]{3,2,1,0:T(8,128)(2,1)S(1)}, u32[]{:S(2)}, u32[]{:S(2)}) %all-to-all-start.1) | async-done | bytes 2097184 | tf_op jit(solution)/shard_map/all_to_all | solution.py:9
  293.0 0.2 copy.7
  293.1 5.3 %pad_maximum_fusion = bf16[12288,128]{1,0:T(8,128)(2,1)S(1)} fusion(bf16[8192,128]{1,0:T(8,128)(2,1)S(1)} %bitcast.63, bf16[4096,128]{1,0:T(8,128)(2,1)} %bitcast.62), kind=kLoop, calls=%fused_computation.5 | loop fusion | flops 6291456 | bytes 6291456 | tf_op jit(solution)/shard_map/concatenate | solution.py:53
  298.5 57.8 %gather_fusion.1 = bf16[16384,128]{1,0:T(8,128)(2,1)} fusion(bf16[12288,128]{1,0:T(8,128)(2,1)S(1)} %pad_maximum_fusion, s32[16384]{0:T(1024)S(1)} %broadcast_clamp_fusion), kind=kCustom, calls=%fused_computation.1 | custom fusion | bytes 8454144 | tf_op jit(solution)/shard_map/jit(_take)/gather | solution.py:54
  356.3 5.9 %fusion.31 = bf16[4,64,128]{2,1,0:T(8,128)(2,1)} fusion(bf16[4,4096,128]{2,1,0:T(8,128)(2,1)} %bitcast.65, pred[4,4096]{1,0:T(4,128)(4,1)S(1)} %compare_and_fusion, bf16[6,64,4096]{2,1,0:T(8,128)(2,1)} %param.7, f32[7,64,128]{2,1,0:T(8,128)} %param.5, f32[4,64]{1,0:T(4,128)S(1)} %slice.62), kind=kOutput, calls=%fused_computation.18 | convolution fusion | flops 270630912 | bytes 6505472 | tf_op jit(solution)/shard_map/fik,fkr->fir/dot_general | solution.py:29
  362.3 77.2 %all-gather.8.cloned.1.call-done = bf16[4,4096,128]{2,1,0:T(8,128)(2,1)} async-done(((bf16[4,64,128]{2,1,0:T(8,128)(2,1)}), bf16[4,4096,128]{2,1,0:T(8,128)(2,1)}) %all-gather.8.cloned.1.call-update) | async-done | bytes 4194320 | tf_op jit(solution)/shard_map/all_gather | solution.py:22
  439.5 3.7 fusion.13
  443.1 0.7 multiply_reduce_fusion
  443.8 8.4 %psum.7 = f32[7,64]{1,0:T(8,128)S(1)} all-reduce(f32[7,64]{1,0:T(8,128)S(1)} %get-tuple-element.2), channel_id=1, replica_groups=mesh['leaf'=64,'panel'=4] {'panel'}, use_global_device_ids=true, to_apply=%region_1.2 | all-reduce | flops 448 | bytes 3584 | tf_op jit(solution)/shard_map/psum | solution.py:57
  452.2 0.6 broadcast_multiply_fusion
  (27 shorter events, 0.5 us)
Async XLA Ops:
  7.2 94.9 %copy-start.1 = (s32[6,32]{1,0:T(8,128)S(1)}, s32[6,32]{1,0:T(8,128)}, u32[]{:S(2)}) copy-start(s32[6,32]{1,0:T(8,128)} %param.8) | copy-start | bytes 2308
  7.2 85.2 %all-gather.4.cloned.1.call-start = ((), (), s32[]{:S(2)}) async-start(), calls=%async_computation.2 | async-start | bytes 1064960 | tf_op jit(solution)/shard_map/all_gather | solution.py:22
  95.3 34.9 %all-to-all-start = ((bf16[64,1,64,128]{3,2,1,0:T(8,128)(2,1)}), bf16[64,1,64,128]{3,2,1,0:T(8,128)(2,1)S(1)}, u32[]{:S(2)}, u32[]{:S(2)}) async-start(bf16[64,1,64,128]{3,2,1,0:T(8,128)(2,1)} %stack.4), calls=%async_computation | async-start | bytes 2097152 | tf_op jit(solution)/shard_map/all_to_all | solution.py:9
  102.0 130.6 %all-gather.6.cloned.1.call-start = ((), (), s32[]{:S(2)}) async-start(), calls=%async_computation.3 | async-start | bytes 2129920 | tf_op jit(solution)/shard_map/all_gather | solution.py:22
  130.2 24.0 %copy-start = (bf16[64,1,64,128]{3,2,1,0:T(8,128)(2,1)}, bf16[64,1,64,128]{3,2,1,0:T(8,128)(2,1)S(1)}, u32[]{:S(2)}) copy-start(bf16[64,1,64,128]{3,2,1,0:T(8,128)(2,1)S(1)} %all-to-all-done) | copy-start | bytes 3145732
  236.9 56.1 %all-to-all-start.1 = ((bf16[64,2,64,128]{3,2,1,0:T(8,128)(2,1)}), bf16[64,2,64,128]{3,2,1,0:T(8,128)(2,1)S(1)}, u32[]{:S(2)}, u32[]{:S(2)}) async-start(bf16[64,2,64,128]{3,2,1,0:T(8,128)(2,1)} %stack.5), calls=%async_computation.1 | async-start | bytes 4194304 | tf_op jit(solution)/shard_map/all_to_all | solution.py:9
  243.3 196.2 %all-gather.8.cloned.1.call-start = ((), (), s32[]{:S(2)}) async-start(), calls=%async_computation.4 | async-start | bytes 4259840 | tf_op jit(solution)/shard_map/all_gather | solution.py:22
Sparse Core Ops, SparseCore 0:
  11.3 80.9 all-gather.3
  157.7 74.8 all-gather.5
  362.4 77.0 all-gather.7
